TPU v7x, 32 devices: a whole 2x2x4 slice. The times are simulated.
32 devices in a mesh: row: 4 (over z), col: 2 (over x), pole: 4 (over y, core).
Axes of the slice: x: 2, y: 2, z: 4, core: 2. Of those that a mesh axis runs over, the one named last changes fastest.
Arguments:
- window: bfloat16 [4, 8192, 8192], P('pole', 'col', 'row'), may hold values from -6 to 6
- panels: bfloat16 [4, 2, 8192, 256], P('pole', 'col', 'row'), may hold values from -0.0625 to 0.0625
- row_map: int32 [3, 8192], P(None, 'row'), may hold values from 0 to 8191, as said below
- panel_root: int32 [4, 3], P('pole'), may hold values from 0 to 1
- upper_blocks: bfloat16 [4, 3, 256, 256], P('pole', None, 'row'), may hold values from -0.375 to 0.375
- diag_inverse: float32 [4, 3, 256, 256], P('pole', None, 'row'), may hold values from -6 to 6
- weights: float32 [4], replicated, may hold values from 0.25 to 1
- pole_order: int32 [4], P('pole'), may hold values from 0 to 3, each once
Outputs:
- inv_columns: float32 [3, 2, 4096, 256], P(None, 'col', ('row', 'pole'))
- inv_diag: float32 [3, 256, 256], P(None, ('row', 'pole'))
Inputs may be any that keep to these rules, and one draw needn't show every extreme that they name: row_map[k] permutes the positions inside each aligned group of 1024 consecutive positions. `pole_order`: each of the 4 poles appears once.
All inputs are finite; a program needn't handle non-finite values.
Results may differ from a plain program's by a relative error of at most 0.0003.
Values may be sent and summed in bfloat16 or wider, within the bound.
A program may use at most 128 MiB of HBM per device.

v0:
```python
import jax
import jax.numpy as jnp
from jax import lax
from jax.sharding import PartitionSpec as P

NS = 3


def precise(left, right):
    return jnp.dot(left, right, precision=lax.Precision.HIGHEST, preferred_element_type=jnp.float32)


def pair_index(current, earlier):
    return current * (current - 1) // 2 + earlier


def inverse_block(diagonals, crossed, first, second):
    if first == second:
        return diagonals[first]
    if first < second:
        return crossed[first, second]
    return crossed[second, first].T


def window_term(window_block, aligned):
    return jnp.dot(window_block, aligned, preferred_element_type=jnp.float32)


def shards(window, panels, row_map, panel_root, upper_blocks, diag_inverse, weights, pole_order):
    window_block = window[0]
    panel_slab = panels[0, 0]
    pole_roots = panel_root[0]
    band_rows = panel_slab.shape[0]
    group_rows = window_block.shape[0] // lax.axis_size("row")
    row_index = lax.axis_index("row")
    col_index = lax.axis_index("col")
    gathered_upper, gathered_inverse = (
        lax.all_gather(upper_blocks.astype(jnp.float32), "row", axis=2, tiled=True).astype(
            upper_blocks.dtype
        ),
        lax.all_gather(diag_inverse, "row", axis=2, tiled=True),
    )
    factors = gathered_upper[0].astype(jnp.float32)
    inverses = gathered_inverse[0]
    share_rows = inverses.shape[1] // lax.axis_size("row")
    slot_panels = lax.all_gather(panels, "col", axis=1, tiled=True)[0]
    pole_weight = jnp.sum(jnp.where(jnp.arange(weights.shape[0]) == pole_order[0], weights, 0.0))
    columns = []
    diagonals = []
    crossed = {}
    for current in range(NS):
        received = lax.dynamic_index_in_dim(slot_panels, pole_roots[current], 0, keepdims=False)
        aligned = jnp.take(received, row_map[current] - row_index * band_rows, axis=0)
        own_rows = lax.dynamic_slice_in_dim(aligned, col_index * group_rows, group_rows, 0).astype(
            jnp.float32
        )
        partials = [precise(columns[earlier].T, own_rows) for earlier in range(current)]
        window_sum = lax.psum_scatter(
            window_term(window_block, aligned), "row", scatter_dimension=0, tiled=True
        )
        y_window = window_sum
        for earlier in range(current):
            y_window = y_window + precise(columns[earlier], factors[pair_index(current, earlier)])
        congruence = precise(own_rows.T, y_window)
        stacked = lax.psum(jnp.stack(partials + [congruence]), ("row", "col"))
        summed_cross = stacked[:current]
        summed_own = stacked[current]
        y_blocks = []
        for earlier in range(current):
            block_sum = summed_cross[earlier]
            for other_node in range(current):
                block_sum = block_sum + precise(
                    inverse_block(diagonals, crossed, earlier, other_node),
                    factors[pair_index(current, other_node)],
                )
            y_blocks.append(block_sum)
        diagonal = inverses[current] + summed_own
        for earlier in range(current):
            diagonal = diagonal + precise(
                factors[pair_index(current, earlier)].T, y_blocks[earlier]
            )
            crossed[earlier, current] = -y_blocks[earlier]
        columns.append(-y_window)
        diagonals.append(diagonal)
    column_terms = jnp.stack(columns) * pole_weight
    diagonal_terms = (
        jnp.stack(
            [
                lax.dynamic_slice_in_dim(diagonal, row_index * share_rows, share_rows, 0)
                for diagonal in diagonals
            ]
        )
        * pole_weight
    )
    summed_columns, summed_diagonals = (
        lax.psum_scatter(column_terms, "pole", scatter_dimension=1, tiled=True),
        lax.psum_scatter(diagonal_terms, "pole", scatter_dimension=1, tiled=True),
    )
    return (summed_columns[:, None], summed_diagonals)


def solution(mesh):
    return jax.shard_map(
        shards,
        mesh=mesh,
        in_specs=(
            P("pole", "col", "row"),
            P("pole", "col", "row", None),
            P(None, "row"),
            P("pole", None),
            P("pole", None, "row", None),
            P("pole", None, "row", None),
            P(),
            P("pole"),
        ),
        out_specs=(P(None, "col", ("row", "pole"), None), P(None, ("row", "pole"), None)),
        check_vma=False,
    )
```

profile of v0, /device:TPU:0, one launch (start us, length us, event | category | flops | bytes accessed | tf_op | source)
XLA Modules:
  0.0 490.8 jit_solution(11846383781759528025)
XLA Ops:
  7.2 0.0 all-gather.2.cloned.1.call-start
  7.2 0.7 all-gather.2.cloned.1.call-update
  7.9 0.0 reduce-scatter.6.cloned.1.call-start
  7.9 1.4 fusion.45
  15.1 0.9 slice_subtract_fusion.1
  16.0 29.3 %all-gather.2.cloned.1.call-done = bf16[1,2,2048,256]{3,2,0,1:T(8,128)(2,1)} async-done(((bf16[1,1,2048,256]{3,2,0,1:T(8,128)(2,1)}), bf16[1,2,2048,256]{3,2,0,1:T(8,128)(2,1)}) %all-gather.2.cloned.1.call-update) | async-done | bytes 2097168 | tf_op jit(solution)/shard_map/all_gather | solution.py:46
  45.4 2.2 dynamic-slice_bitcast_fusion.1
  47.6 9.0 %gather_fusion = bf16[2048,256]{1,0:T(8,128)(2,1)} fusion(bf16[2048,256]{1,0:T(8,128)(2,1)S(1)} %get-tuple-element.12, s32[2048]{0:T(1024)S(1)} %fusion.35), kind=kCustom, calls=%fused_computation.clone | custom fusion | bytes 2105344 | tf_op jit(solution)/shard_map/jit(_take)/gather | solution.py:53
  56.6 1.5 broadcast_select_fusion.2
  58.1 10.5 %fusion.6 = f32[4096,256]{0,1:T(8,128)} fusion(bf16[2048,256]{1,0:T(8,128)(2,1)S(1)} %broadcast_select_fusion.2, bf16[1,4096,2048]{2,1,0:T(8,128)(2,1)} %param.10), kind=kOutput, calls=%fused_computation.9 | convolution fusion | flops 4294967296 | bytes 22020096 | tf_op jit(solution)/shard_map/dot_general | solution.py:26
  68.6 0.0 reduce-scatter.6.cloned.1.call-update
  68.6 0.0 reduce-scatter.8.cloned.1.call-start
  68.7 7.5 %gather_fusion.1 = bf16[2048,256]{1,0:T(8,128)(2,1)S(1)} fusion(bf16[2048,256]{1,0:T(8,128)(2,1)S(1)} %get-tuple-element.10, s32[2048]{0:T(1024)S(1)} %fusion.36), kind=kCustom, calls=%fused_computation.1.clone | custom fusion | bytes 2105344 | tf_op jit(solution)/shard_map/jit(_take)/gather | solution.py:53
  76.2 0.4 broadcast_select_fusion.1
  76.7 10.6 %fusion.9 = f32[4096,256]{0,1:T(8,128)} fusion(bf16[2048,256]{1,0:T(8,128)(2,1)S(1)} %broadcast_select_fusion.1, bf16[1,4096,2048]{2,1,0:T(8,128)(2,1)} %param.10), kind=kOutput, calls=%fused_computation.10 | convolution fusion | flops 4294967296 | bytes 22020096 | tf_op jit(solution)/shard_map/dot_general | solution.py:26
  87.3 0.0 reduce-scatter.8.cloned.1.call-update
  87.3 0.0 reduce-scatter.10.cloned.1.call-start
  87.4 7.5 %gather_fusion.2 = bf16[2048,256]{1,0:T(8,128)(2,1)S(1)} fusion(bf16[2048,256]{1,0:T(8,128)(2,1)S(1)} %get-tuple-element.11, s32[2048]{0:T(1024)S(1)} %fusion.37), kind=kCustom, calls=%fused_computation.2.clone | custom fusion | bytes 2105344 | tf_op jit(solution)/shard_map/jit(_take)/gather | solution.py:53
  94.9 0.4 broadcast_select_fusion
  95.3 10.6 %fusion.12 = f32[4096,256]{0,1:T(8,128)} fusion(bf16[2048,256]{1,0:T(8,128)(2,1)S(1)} %broadcast_select_fusion, bf16[1,4096,2048]{2,1,0:T(8,128)(2,1)} %param.10), kind=kOutput, calls=%fused_computation.11 | convolution fusion | flops 4294967296 | bytes 22020096 | tf_op jit(solution)/shard_map/dot_general | solution.py:26
  105.9 0.0 reduce-scatter.10.cloned.1.call-update
  105.9 0.0 all-reduce.3.cloned.1.call-start
  106.0 0.8 copy-done.11
  106.8 20.3 %all_gather.10 = bf16[1,3,256,256]{3,2,1,0:T(8,128)(2,1)S(1)} all-gather(bf16[1,3,64,256]{3,2,1,0:T(8,128)(2,1)S(1)} %copy-done.11), channel_id=1, replica_groups=mesh['row'=4,'col'=2,'pole'=4] {'row'}, dimensions={2}, use_global_device_ids=true | all-gather | bytes 491520 | tf_op jit(solution)/shard_map/all_gather | solution.py:38
  127.2 24.6 %reduce-scatter.6.cloned.1.call-done = f32[1024,256]{0,1:T(8,128)} async-done(((f32[4096,256]{0,1:T(8,128)}), f32[1024,256]{0,1:T(8,128)}) %reduce-scatter.6.cloned.1.call-update) | async-done | bytes 1048592 | tf_op jit(solution)/shard_map/reduce_scatter | solution.py:58
  151.8 79.5 %reduce-scatter.8.cloned.1.call-done = f32[1024,256]{0,1:T(8,128)} async-done(((f32[4096,256]{0,1:T(8,128)}), f32[1024,256]{0,1:T(8,128)}) %reduce-scatter.8.cloned.1.call-update) | async-done | bytes 1048592 | tf_op jit(solution)/shard_map/reduce_scatter | solution.py:58
  231.3 2.2 convolution_add_fusion.2
  233.6 2.5 convolution_bitcast_fusion.6
  236.1 1.3 convolution_bitcast_fusion.4
  237.4 73.4 %reduce-scatter.10.cloned.1.call-done = f32[1024,256]{0,1:T(8,128)} async-done(((f32[4096,256]{0,1:T(8,128)}), f32[1024,256]{0,1:T(8,128)}) %reduce-scatter.10.cloned.1.call-update) | async-done | bytes 1048592 | tf_op jit(solution)/shard_map/reduce_scatter | solution.py:58
  310.8 2.1 convolution_add_fusion.1
  312.9 0.7 convolution_add_fusion
  313.7 0.8 convolution_bitcast_fusion.3
  314.4 0.6 convolution_bitcast_fusion.7
  315.1 0.8 pad_maximum_fusion.1
  315.9 0.6 convolution_bitcast_fusion.5
  316.6 0.9 pad_maximum_fusion
  317.5 1.5 convolution_bitcast_fusion.8
  319.0 0.0 all-reduce.3.cloned.1.call-update
  319.0 0.0 reduce-scatter.12.cloned.1.call-start
  319.7 0.6 fusion.44
  320.3 0.1 negate_bitcast_fusion.2
  320.4 0.2 negate_bitcast_fusion
  320.6 0.0 copy-start.10
  320.6 2.6 maximum_multiply_fusion
  323.2 0.0 reduce-scatter.12.cloned.1.call-update
  323.2 0.0 reduce-scatter.14.cloned.1.call-start
  323.3 31.1 %all_gather.11 = f32[1,3,256,256]{3,2,1,0:T(8,128)S(1)} all-gather(f32[1,3,64,256]{3,2,1,0:T(8,128)S(1)} %copy-done.10), channel_id=1, replica_groups=mesh['row'=4,'col'=2,'pole'=4] {'row'}, dimensions={2}, use_global_device_ids=true | all-gather | bytes 983040 | tf_op jit(solution)/shard_map/all_gather | solution.py:41
  354.4 67.3 %all-reduce.3.cloned.1.call-done = (f32[3,256,256]{2,1,0:T(8,128)}, f32[2,256,256]{2,1,0:T(8,128)}, f32[1,256,256]{2,1,0:T(8,128)}) async-done(((f32[3,256,256]{2,1,0:T(8,128)}, f32[2,256,256]{2,1,0:T(8,128)}, f32[1,256,256]{2,1,0:T(8,128)}), (f32[3,256,256]{2,1,0:T(8,128)}, f32[2,256,256]{2,1,0:T(8,128)}, f32[1,256,256]{2,1,0:T(8,128)})) %all-reduce.3.cloned.1.call-update) | async-done | bytes 1572880 | tf_op jit(solution)/shard_map/psum | solution.py:65
  421.8 0.9 fusion.34
  422.7 1.0 slice_bitcast_fusion.2
  423.6 1.3 convolution_add_fusion.6
  424.9 1.3 convolution_add_fusion.7
  426.3 0.3 convolution_add_fusion.5
  426.5 0.3 convolution_bitcast_fusion.1
  426.9 1.3 convolution_add_fusion.4
  428.2 0.3 fusion.15
  428.5 0.3 convolution_add_fusion.3
  428.8 0.3 convolution_bitcast_fusion
  429.2 1.3 maximum_multiply_fusion.1
  430.4 0.0 reduce-scatter.14.cloned.1.call-update
  430.5 30.6 %reduce-scatter.12.cloned.1.call-done = f32[3,256,256]{1,2,0:T(8,128)} async-done(((f32[3,1024,256]{1,2,0:T(8,128)}), f32[3,256,256]{1,2,0:T(8,128)}) %reduce-scatter.12.cloned.1.call-update) | async-done | bytes 786448 | tf_op jit(solution)/shard_map/reduce_scatter | solution.py:96
  461.1 2.3 copy.18
  463.4 20.6 %reduce-scatter.14.cloned.1.call-done = f32[3,16,256]{2,1,0:T(8,128)} async-done(((f32[3,64,256]{2,1,0:T(8,128)}), f32[3,16,256]{2,1,0:T(8,128)}) %reduce-scatter.14.cloned.1.call-update) | async-done | bytes 49168 | tf_op jit(solution)/shard_map/reduce_scatter | solution.py:97
  (32 shorter events, 0.2 us)
Async XLA Ops:
  7.2 38.2 %all-gather.2.cloned.1.call-start = ((), (), s32[]{:S(2)}) async-start(), calls=%async_computation.5 | async-start | bytes 3145728 | tf_op jit(solution)/shard_map/all_gather | solution.py:46
  7.9 143.9 %reduce-scatter.6.cloned.1.call-start = ((), (), s32[]{:S(2)}) async-start(), calls=%async_computation.6 | async-start | bytes 5242880 | tf_op jit(solution)/shard_map/reduce_scatter | solution.py:58
  58.1 10.5 %copy-start.5 = (bf16[2048,256]{1,0:T(8,128)(2,1)}, bf16[2048,256]{1,0:T(8,128)(2,1)S(1)}, u32[]{:S(2)}) copy-start(bf16[2048,256]{1,0:T(8,128)(2,1)S(1)} %broadcast_select_fusion.2) | copy-start | bytes 3145732
  68.6 162.7 %reduce-scatter.8.cloned.1.call-start = ((), (), s32[]{:S(2)}) async-start(), calls=%async_computation.7 | async-start | bytes 5242880 | tf_op jit(solution)/shard_map/reduce_scatter | solution.py:58
  76.7 10.6 %copy-start.3 = (bf16[2048,256]{1,0:T(8,128)(2,1)}, bf16[2048,256]{1,0:T(8,128)(2,1)S(1)}, u32[]{:S(2)}) copy-start(bf16[2048,256]{1,0:T(8,128)(2,1)S(1)} %broadcast_select_fusion.1) | copy-start | bytes 3145732
  87.3 223.5 %reduce-scatter.10.cloned.1.call-start = ((), (), s32[]{:S(2)}) async-start(), calls=%async_computation.8 | async-start | bytes 5242880 | tf_op jit(solution)/shard_map/reduce_scatter | solution.py:58
  95.3 140.8 %copy-start.1 = (bf16[2048,256]{1,0:T(8,128)(2,1)}, bf16[2048,256]{1,0:T(8,128)(2,1)S(1)}, u32[]{:S(2)}) copy-start(bf16[2048,256]{1,0:T(8,128)(2,1)S(1)} %broadcast_select_fusion) | copy-start | bytes 3145732
  105.9 0.9 copy-start.11
  105.9 315.8 %all-reduce.3.cloned.1.call-start = ((), (), s32[]{:S(2)}) async-start(), calls=%async_computation.11 | async-start | bytes 3145728 | tf_op jit(solution)/shard_map/psum | solution.py:65
  151.8 159.0 %copy-start = (f32[1024,256]{0,1:T(8,128)S(1)}, f32[1024,256]{0,1:T(8,128)}, u32[]{:S(2)}) copy-start(f32[1024,256]{0,1:T(8,128)} %reduce-scatter.6.cloned.1.call-done) | copy-start | bytes 3145732
  310.8 2.8 copy-start.2
  310.8 3.6 copy-start.4
  312.9 2.2 copy-start.8
  312.9 3.7 copy-start.7
  313.6 3.9 copy-start.6
  315.1 4.6 copy-start.12
  319.0 142.1 %reduce-scatter.12.cloned.1.call-start = ((), (), s32[]{:S(2)}) async-start(), calls=%async_computation.9 | async-start | bytes 3932160 | tf_op jit(solution)/shard_map/reduce_scatter | solution.py:96
  320.6 2.6 copy-start.10
  323.2 160.7 %reduce-scatter.14.cloned.1.call-start = ((), (), s32[]{:S(2)}) async-start(), calls=%async_computation.10 | async-start | bytes 245760 | tf_op jit(solution)/shard_map/reduce_scatter | solution.py:97
  421.8 6.5 %copy-start.9 = (f32[2,256,256]{2,1,0:T(8,128)S(1)}, f32[2,256,256]{2,1,0:T(8,128)}, u32[]{:S(2)}) copy-start(f32[2,256,256]{2,1,0:T(8,128)} %get-tuple-element.8) | copy-start | bytes 1572868
Sparse Core Ops, SparseCore 0:
  9.5 35.8 all-gather.1
  68.8 82.9 reduce-scatter.5
  154.1 77.2 reduce-scatter.7
  233.5 77.2 reduce-scatter.9
  319.2 102.5 all-reduce.2
  424.1 36.9 reduce-scatter.11
  464.1 19.7 reduce-scatter.13
where the time goes:
time: 491 us
  waiting for transfers between devices  326 us (66%)
  blocking collectives  51.5 us (10%)
  matrix products  49.5 us (10%)
  local copies, waits for them, and re-layouts  31.8 us (6%)
  between operations  20.9 us (4%)
  other arithmetic  10.7 us (2%)
    reduce_scatter x3, waiting for transfers between devices, shards(): lax.psum_scatter(window_term(window_block, aligned), 'row', scatter_dimen...  178 us
    psum x1, waiting for transfers between devices, shards(): stacked = lax.psum(jnp.stack(partials + [congruence]), ('row', 'col'))  67.3 us
    dot_general x3, matrix products, window_term(): return jnp.dot(window_block, aligned, preferred_element_type=jnp.float32)  31.7 us
    all_gather x1, blocking collectives, shards(): lax.all_gather(diag_inverse, 'row', axis=2, tiled=True)  31.1 us
    reduce_scatter x1, waiting for transfers between devices, shards(): lax.psum_scatter(column_terms, 'pole', scatter_dimension=1, tiled=True)  30.6 us
    all_gather x1, waiting for transfers between devices, shards(): slot_panels = lax.all_gather(panels, 'col', axis=1, tiled=True)[0]  29.3 us
    gather x3, local copies, waits for them, and re-layouts, shards(): jnp.take(received, row_map[current] - row_index * band_rows, axis=0)  24 us
    reduce_scatter x1, waiting for transfers between devices, shards(): lax.psum_scatter(diagonal_terms, 'pole', scatter_dimension=1, tiled=True)  20.6 us
  transfers between devices with their start and end apart: 7, of which 7 were waited for; matrix products, arithmetic and copies ran while one was open for 12% of the time, Pallas kernels for 0%

commit v1 on v0

--- a/solution.py
+++ b/solution.py
@@ -1,9 +1,19 @@
+import functools
 import jax
 import jax.numpy as jnp
 from jax import lax
 from jax.sharding import PartitionSpec as P
 
 NS = 3
+
+
+def proceed_tables_by_axis(xx, shard_axis, lane_axis):
+    for q in (shard_axis, lane_axis):
+        xx = lax.psum(xx, axis_name=q)
+    return xx
+
+
+finish_forms = functools.partial(proceed_tables_by_axis, shard_axis="col", lane_axis="row")
 
 
 def precise(left, right):
@@ -62,7 +72,7 @@
         for earlier in range(current):
             y_window = y_window + precise(columns[earlier], factors[pair_index(current, earlier)])
         congruence = precise(own_rows.T, y_window)
-        stacked = lax.psum(jnp.stack(partials + [congruence]), ("row", "col"))
+        stacked = finish_forms(jnp.stack(partials + [congruence]))
         summed_cross = stacked[:current]
         summed_own = stacked[current]
         y_blocks = []

time: 491 us -> 523 us (1.065)
  waiting for transfers between devices: 326 us -> 359 us
    psum x1 -> x2, waiting for transfers between devices: 67.3 us -> 99.8 us  [proceed_tables_by_axis(): xx = lax.psum(xx, axis_name=q)]
  transfers between devices with their start and end apart: 7 -> 8, of which waited for: 7 -> 8; matrix products, arithmetic and copies ran while one was open for 12% -> 11% of each run, Pallas kernels for 0% -> 0%
where the time goes in v1:
time: 523 us; the launch traced here: 522 us
  waiting for transfers between devices  359 us (69%)
  blocking collectives  50.1 us (10%)
  matrix products  49.6 us (9%)
  local copies, waits for them, and re-layouts  31.8 us (6%)
  between operations  20.9 us (4%)
  other arithmetic  10.9 us (2%)
    reduce_scatter x3, waiting for transfers between devices, shards(): lax.psum_scatter(window_term(window_block, aligned), 'row', scatter_dimen...  178 us
    psum x2, waiting for transfers between devices, proceed_tables_by_axis(): xx = lax.psum(xx, axis_name=q)  99.8 us
    dot_general x3, matrix products, window_term(): return jnp.dot(window_block, aligned, preferred_element_type=jnp.float32)  31.7 us
    reduce_scatter x1, waiting for transfers between devices, shards(): lax.psum_scatter(column_terms, 'pole', scatter_dimension=1, tiled=True)  30.6 us
    all_gather x1, blocking collectives, shards(): lax.all_gather(diag_inverse, 'row', axis=2, tiled=True)  29.8 us
    all_gather x1, waiting for transfers between devices, shards(): slot_panels = lax.all_gather(panels, 'col', axis=1, tiled=True)[0]  29.3 us
    gather x3, local copies, waits for them, and re-layouts, shards(): jnp.take(received, row_map[current] - row_index * band_rows, axis=0)  24 us
    reduce_scatter x1, waiting for transfers between devices, shards(): lax.psum_scatter(diagonal_terms, 'pole', scatter_dimension=1, tiled=True)  20.5 us
  transfers between devices with their start and end apart: 8, of which 8 were waited for; matrix products, arithmetic and copies ran while one was open for 11% of the time, Pallas kernels for 0%

profile of v1, /device:TPU:0, one launch (start us, length us, event | category | flops | bytes accessed | tf_op | source)
XLA Modules:
  0.0 522.2 jit_solution(18153262156397842658)
XLA Ops:
  7.2 0.0 all-gather.2.cloned.1.call-start
  7.2 0.7 all-gather.2.cloned.1.call-update
  7.9 0.0 reduce-scatter.6.cloned.1.call-start
  7.9 1.4 fusion.45
  15.1 0.9 slice_subtract_fusion.1
  16.0 29.3 %all-gather.2.cloned.1.call-done = bf16[1,2,2048,256]{3,2,0,1:T(8,128)(2,1)} async-done(((bf16[1,1,2048,256]{3,2,0,1:T(8,128)(2,1)}), bf16[1,2,2048,256]{3,2,0,1:T(8,128)(2,1)}) %all-gather.2.cloned.1.call-update) | async-done | bytes 2097168 | tf_op jit(solution)/shard_map/all_gather | solution.py:56
  45.4 2.3 dynamic-slice_bitcast_fusion.1
  47.6 9.0 %gather_fusion = bf16[2048,256]{1,0:T(8,128)(2,1)} fusion(bf16[2048,256]{1,0:T(8,128)(2,1)S(1)} %get-tuple-element.15, s32[2048]{0:T(1024)S(1)} %fusion.35), kind=kCustom, calls=%fused_computation.clone | custom fusion | bytes 2105344 | tf_op jit(solution)/shard_map/jit(_take)/gather | solution.py:63
  56.6 1.5 broadcast_select_fusion.2
  58.1 10.5 %fusion.6 = f32[4096,256]{0,1:T(8,128)} fusion(bf16[2048,256]{1,0:T(8,128)(2,1)S(1)} %broadcast_select_fusion.2, bf16[1,4096,2048]{2,1,0:T(8,128)(2,1)} %param.10), kind=kOutput, calls=%fused_computation.9 | convolution fusion | flops 4294967296 | bytes 22020096 | tf_op jit(solution)/shard_map/dot_general | solution.py:36
  68.6 0.0 reduce-scatter.6.cloned.1.call-update
  68.7 0.0 reduce-scatter.8.cloned.1.call-start
  68.7 7.5 %gather_fusion.1 = bf16[2048,256]{1,0:T(8,128)(2,1)S(1)} fusion(bf16[2048,256]{1,0:T(8,128)(2,1)S(1)} %get-tuple-element.13, s32[2048]{0:T(1024)S(1)} %fusion.36), kind=kCustom, calls=%fused_computation.1.clone | custom fusion | bytes 2105344 | tf_op jit(solution)/shard_map/jit(_take)/gather | solution.py:63
  76.3 0.4 broadcast_select_fusion.1
  76.7 10.6 %fusion.9 = f32[4096,256]{0,1:T(8,128)} fusion(bf16[2048,256]{1,0:T(8,128)(2,1)S(1)} %broadcast_select_fusion.1, bf16[1,4096,2048]{2,1,0:T(8,128)(2,1)} %param.10), kind=kOutput, calls=%fused_computation.10 | convolution fusion | flops 4294967296 | bytes 22020096 | tf_op jit(solution)/shard_map/dot_general | solution.py:36
  87.3 0.0 reduce-scatter.8.cloned.1.call-update
  87.3 0.0 reduce-scatter.10.cloned.1.call-start
  87.4 7.5 %gather_fusion.2 = bf16[2048,256]{1,0:T(8,128)(2,1)S(1)} fusion(bf16[2048,256]{1,0:T(8,128)(2,1)S(1)} %get-tuple-element.14, s32[2048]{0:T(1024)S(1)} %fusion.37), kind=kCustom, calls=%fused_computation.2.clone | custom fusion | bytes 2105344 | tf_op jit(solution)/shard_map/jit(_take)/gather | solution.py:63
  94.9 0.4 broadcast_select_fusion
  95.4 10.6 %fusion.12 = f32[4096,256]{0,1:T(8,128)} fusion(bf16[2048,256]{1,0:T(8,128)(2,1)S(1)} %broadcast_select_fusion, bf16[1,4096,2048]{2,1,0:T(8,128)(2,1)} %param.10), kind=kOutput, calls=%fused_computation.11 | convolution fusion | flops 4294967296 | bytes 22020096 | tf_op jit(solution)/shard_map/dot_general | solution.py:36
  106.0 0.0 reduce-scatter.10.cloned.1.call-update
  106.0 0.0 all-reduce.7.cloned.1.call-start
  106.0 0.8 copy-done.11
  106.8 20.3 %all_gather.10 = bf16[1,3,256,256]{3,2,1,0:T(8,128)(2,1)S(1)} all-gather(bf16[1,3,64,256]{3,2,1,0:T(8,128)(2,1)S(1)} %copy-done.11), channel_id=1, replica_groups=mesh['row'=4,'col'=2,'pole'=4] {'row'}, dimensions={2}, use_global_device_ids=true | all-gather | bytes 491520 | tf_op jit(solution)/shard_map/all_gather | solution.py:48
  127.2 24.6 %reduce-scatter.6.cloned.1.call-done = f32[1024,256]{0,1:T(8,128)} async-done(((f32[4096,256]{0,1:T(8,128)}), f32[1024,256]{0,1:T(8,128)}) %reduce-scatter.6.cloned.1.call-update) | async-done | bytes 1048592 | tf_op jit(solution)/shard_map/reduce_scatter | solution.py:68
  151.8 79.6 %reduce-scatter.8.cloned.1.call-done = f32[1024,256]{0,1:T(8,128)} async-done(((f32[4096,256]{0,1:T(8,128)}), f32[1024,256]{0,1:T(8,128)}) %reduce-scatter.8.cloned.1.call-update) | async-done | bytes 1048592 | tf_op jit(solution)/shard_map/reduce_scatter | solution.py:68
  231.3 2.2 convolution_add_fusion.2
  233.6 2.5 convolution_bitcast_fusion.6
  236.1 1.3 convolution_bitcast_fusion.4
  237.5 73.4 %reduce-scatter.10.cloned.1.call-done = f32[1024,256]{0,1:T(8,128)} async-done(((f32[4096,256]{0,1:T(8,128)}), f32[1024,256]{0,1:T(8,128)}) %reduce-scatter.10.cloned.1.call-update) | async-done | bytes 1048592 | tf_op jit(solution)/shard_map/reduce_scatter | solution.py:68
  310.8 2.1 convolution_add_fusion.1
  312.9 0.7 convolution_add_fusion
  313.7 0.8 convolution_bitcast_fusion.3
  314.5 0.6 convolution_bitcast_fusion.7
  315.1 0.8 pad_maximum_fusion.1
  316.0 0.6 convolution_bitcast_fusion.5
  316.6 0.9 pad_maximum_fusion
  317.6 1.5 convolution_bitcast_fusion.8
  319.0 0.0 all-reduce.7.cloned.1.call-update
  319.1 0.0 all-reduce.5.cloned.1.call-start
  319.1 52.2 %all-reduce.7.cloned.1.call-done = (f32[3,256,256]{2,1,0:T(8,128)}, f32[2,256,256]{2,1,0:T(8,128)}, f32[1,256,256]{2,1,0:T(8,128)}) async-done(((f32[3,256,256]{2,1,0:T(8,128)}, f32[2,256,256]{2,1,0:T(8,128)}, f32[1,256,256]{2,1,0:T(8,128)}), (f32[3,256,256]{2,1,0:T(8,128)}, f32[2,256,256]{2,1,0:T(8,128)}, f32[1,256,256]{2,1,0:T(8,128)})) %all-reduce.7.cloned.1.call-update) | async-done | bytes 1572880 | tf_op jit(solution)/shard_map/psum | solution.py:12
  371.3 0.0 all-reduce.5.cloned.1.call-update
  371.3 0.0 reduce-scatter.12.cloned.1.call-start
  372.0 0.6 fusion.44
  372.6 0.1 negate_bitcast_fusion.2
  372.7 0.2 negate_bitcast_fusion
  372.9 2.6 maximum_multiply_fusion
  375.6 0.0 reduce-scatter.14.cloned.1.call-start
  375.6 29.8 %all_gather.11 = f32[1,3,256,256]{3,2,1,0:T(8,128)S(1)} all-gather(f32[1,3,64,256]{3,2,1,0:T(8,128)S(1)} %copy-done.10), channel_id=1, replica_groups=mesh['row'=4,'col'=2,'pole'=4] {'row'}, dimensions={2}, use_global_device_ids=true | all-gather | bytes 983040 | tf_op jit(solution)/shard_map/all_gather | solution.py:51
  405.5 47.7 %all-reduce.5.cloned.1.call-done = (f32[3,256,256]{2,1,0:T(8,128)}, f32[2,256,256]{2,1,0:T(8,128)}, f32[1,256,256]{2,1,0:T(8,128)}) async-done(((f32[3,256,256]{2,1,0:T(8,128)}, f32[2,256,256]{2,1,0:T(8,128)}, f32[1,256,256]{2,1,0:T(8,128)}), (f32[3,256,256]{2,1,0:T(8,128)}, f32[2,256,256]{2,1,0:T(8,128)}, f32[1,256,256]{2,1,0:T(8,128)})) %all-reduce.5.cloned.1.call-update) | async-done | bytes 1572880 | tf_op jit(solution)/shard_map/psum | solution.py:12
  453.2 0.9 fusion.34
  454.1 1.0 slice_bitcast_fusion.2
  455.0 1.3 convolution_add_fusion.6
  456.4 1.3 convolution_add_fusion.7
  457.7 0.3 convolution_add_fusion.5
  457.9 0.3 convolution_bitcast_fusion.1
  458.3 1.3 convolution_add_fusion.4
  459.6 0.3 fusion.15
  460.0 0.3 convolution_add_fusion.3
  460.2 0.3 convolution_bitcast_fusion
  460.6 1.3 maximum_multiply_fusion.1
  461.9 30.6 %reduce-scatter.12.cloned.1.call-done = f32[3,256,256]{1,2,0:T(8,128)} async-done(((f32[3,1024,256]{1,2,0:T(8,128)}), f32[3,256,256]{1,2,0:T(8,128)}) %reduce-scatter.12.cloned.1.call-update) | async-done | bytes 786448 | tf_op jit(solution)/shard_map/reduce_scatter | solution.py:106
  492.6 2.3 copy.18
  494.8 20.5 %reduce-scatter.14.cloned.1.call-done = f32[3,16,256]{2,1,0:T(8,128)} async-done(((f32[3,64,256]{2,1,0:T(8,128)}), f32[3,16,256]{2,1,0:T(8,128)}) %reduce-scatter.14.cloned.1.call-update) | async-done | bytes 49168 | tf_op jit(solution)/shard_map/reduce_scatter | solution.py:107
  (35 shorter events, 0.2 us)
Async XLA Ops:
  7.2 38.2 %all-gather.2.cloned.1.call-start = ((), (), s32[]{:S(2)}) async-start(), calls=%async_computation.5 | async-start | bytes 3145728 | tf_op jit(solution)/shard_map/all_gather | solution.py:56
  7.9 143.9 %reduce-scatter.6.cloned.1.call-start = ((), (), s32[]{:S(2)}) async-start(), calls=%async_computation.6 | async-start | bytes 5242880 | tf_op jit(solution)/shard_map/reduce_scatter | solution.py:68
  58.1 10.5 %copy-start.5 = (bf16[2048,256]{1,0:T(8,128)(2,1)}, bf16[2048,256]{1,0:T(8,128)(2,1)S(1)}, u32[]{:S(2)}) copy-start(bf16[2048,256]{1,0:T(8,128)(2,1)S(1)} %broadcast_select_fusion.2) | copy-start | bytes 3145732
  68.7 162.7 %reduce-scatter.8.cloned.1.call-start = ((), (), s32[]{:S(2)}) async-start(), calls=%async_computation.7 | async-start | bytes 5242880 | tf_op jit(solution)/shard_map/reduce_scatter | solution.py:68
  76.7 10.6 %copy-start.3 = (bf16[2048,256]{1,0:T(8,128)(2,1)}, bf16[2048,256]{1,0:T(8,128)(2,1)S(1)}, u32[]{:S(2)}) copy-start(bf16[2048,256]{1,0:T(8,128)(2,1)S(1)} %broadcast_select_fusion.1) | copy-start | bytes 3145732
  87.3 223.5 %reduce-scatter.10.cloned.1.call-start = ((), (), s32[]{:S(2)}) async-start(), calls=%async_computation.8 | async-start | bytes 5242880 | tf_op jit(solution)/shard_map/reduce_scatter | solution.py:68
  95.4 140.8 %copy-start.1 = (bf16[2048,256]{1,0:T(8,128)(2,1)}, bf16[2048,256]{1,0:T(8,128)(2,1)S(1)}, u32[]{:S(2)}) copy-start(bf16[2048,256]{1,0:T(8,128)(2,1)S(1)} %broadcast_select_fusion) | copy-start | bytes 3145732
  106.0 0.9 copy-start.11
  106.0 265.3 %all-reduce.7.cloned.1.call-start = ((), (), s32[]{:S(2)}) async-start(), calls=%async_computation.12 | async-start | bytes 3145728 | tf_op jit(solution)/shard_map/psum | solution.py:12
  151.8 159.1 %copy-start = (f32[1024,256]{0,1:T(8,128)S(1)}, f32[1024,256]{0,1:T(8,128)}, u32[]{:S(2)}) copy-start(f32[1024,256]{0,1:T(8,128)} %reduce-scatter.6.cloned.1.call-done) | copy-start | bytes 3145732
  310.8 2.8 copy-start.2
  310.8 3.6 copy-start.4
  312.9 2.2 copy-start.8
  312.9 3.7 copy-start.7
  313.7 3.9 copy-start.6
  316.0 56.0 %copy-start.12 = (f32[4]{0:T(128)S(1)}, f32[4]{0:T(128)}, u32[]{:S(2)}) copy-start(f32[4]{0:T(128)} %param.16) | copy-start | bytes 52
  319.1 134.1 %all-reduce.5.cloned.1.call-start = ((), (), s32[]{:S(2)}) async-start(), calls=%async_computation.11 | async-start | bytes 3145728 | tf_op jit(solution)/shard_map/psum | solution.py:12
  371.3 121.2 %reduce-scatter.12.cloned.1.call-start = ((), (), s32[]{:S(2)}) async-start(), calls=%async_computation.9 | async-start | bytes 3932160 | tf_op jit(solution)/shard_map/reduce_scatter | solution.py:106
  372.9 2.7 copy-start.10
  375.6 139.8 %reduce-scatter.14.cloned.1.call-start = ((), (), s32[]{:S(2)}) async-start(), calls=%async_computation.10 | async-start | bytes 245760 | tf_op jit(solution)/shard_map/reduce_scatter | solution.py:107
  453.2 6.4 %copy-start.9 = (f32[2,256,256]{2,1,0:T(8,128)S(1)}, f32[2,256,256]{2,1,0:T(8,128)}, u32[]{:S(2)}) copy-start(f32[2,256,256]{2,1,0:T(8,128)} %get-tuple-element.8) | copy-start | bytes 1572868
Sparse Core Ops, SparseCore 0:
  9.5 35.8 all-gather.1
  68.8 82.9 reduce-scatter.5
  154.1 77.2 reduce-scatter.7
  233.5 77.2 reduce-scatter.9
  319.2 52.0 all-reduce.6
  373.7 79.4 all-reduce.4
  455.7 36.8 reduce-scatter.11
  495.6 19.7 reduce-scatter.13
